TPU v7x, 32 devices: a whole 2x2x4 slice. The times are simulated.
32 devices in a mesh: row: 8 (over y, x, core), col: 4 (over z).
Axes of the slice: x: 2, y: 2, z: 4, core: 2. Of those that a mesh axis runs over, the one named last changes fastest.
Arguments:
- front_matrix: bfloat16 [20480, 20480], P('row', 'col'), may hold values from -37 to 37
- right_samples: bfloat16 [20480, 256], P('col'), may hold values from -0.0390625 to 0.0390625
- left_samples: bfloat16 [20480, 256], P('row'), may hold values from -0.0390625 to 0.0390625
Outputs:
- residual: bfloat16 [20480, 20480], P('row', 'col')
- core_scaled: float32 [256, 256], replicated
All inputs are finite; a program needn't handle non-finite values.
Results may differ from a plain program's by a relative error of at most 0.0035.
Values may be sent and summed in bfloat16 or wider, within the bound.
A program may use at most 128 MiB of HBM per device.

v0:
```python
import jax
import jax.numpy as jnp
from jax import lax
from jax.sharding import PartitionSpec as P

ORDER = 20480


def gram_matrix(sketch):
    return lax.dot_general(
        sketch,
        sketch,
        (((0,), (0,)), ((), ())),
        precision=lax.Precision.HIGHEST,
        preferred_element_type=jnp.float32,
    )


def orthonormal(sketch, gram_total):
    lower_factor = jnp.linalg.cholesky(gram_total)
    return jax.scipy.linalg.solve_triangular(lower_factor, sketch.T, lower=True).T


def core_part(basis_rows, applied):
    return lax.dot_general(
        basis_rows.astype(jnp.float32),
        applied,
        (((0,), (0,)), ((), ())),
        precision=lax.Precision.HIGHEST,
        preferred_element_type=jnp.float32,
    )


def body(front_matrix, right_samples, left_samples):
    sketch_rows = jnp.dot(front_matrix, right_samples, preferred_element_type=jnp.float32)
    sketch_rows = lax.psum(sketch_rows, "col")
    sketch_cols = lax.dot_general(
        front_matrix, left_samples, (((0,), (0,)), ((), ())), preferred_element_type=jnp.float32
    )
    sketch_cols = lax.psum(sketch_cols, "row")
    gram_rows = lax.psum(gram_matrix(sketch_rows), "row")
    gram_cols = lax.psum(gram_matrix(sketch_cols), "col")
    basis_rows = orthonormal(sketch_rows, gram_rows).astype(jnp.bfloat16)
    basis_cols = orthonormal(sketch_cols, gram_cols).astype(jnp.bfloat16)
    applied = jnp.dot(front_matrix, basis_cols, preferred_element_type=jnp.float32)
    applied = lax.psum(applied, "col")
    core_matrix = lax.psum(core_part(basis_rows, applied), "row")
    core_scaled = core_matrix / jnp.sqrt(jnp.float32(ORDER))
    projected = jnp.dot(
        basis_rows.astype(jnp.float32),
        core_matrix,
        precision=lax.Precision.HIGHEST,
        preferred_element_type=jnp.float32,
    ).astype(jnp.bfloat16)
    update = lax.dot_general(
        projected, basis_cols, (((1,), (1,)), ((), ())), preferred_element_type=jnp.float32
    )
    residual = (front_matrix.astype(jnp.float32) - update).astype(jnp.bfloat16)
    return (residual, core_scaled)


def solution(mesh):
    in_specs = (P("row", "col"), P("col", None), P("row", None))
    out_specs = (P("row", "col"), P())
    return jax.shard_map(body, mesh=mesh, in_specs=in_specs, out_specs=out_specs, check_vma=False)
```

profile of v0, /device:TPU:0, one launch (start us, length us, event | category | flops | bytes accessed | tf_op | source)
XLA Modules:
  0.0 564.6 jit_solution(6918856674153980759)
XLA Ops:
  7.2 1.7 copy-done
  8.9 13.5 %fusion.23 = f32[2560,256]{1,0:T(8,128)} fusion(bf16[2560,5120]{1,0:T(8,128)(2,1)} %param.4, bf16[5120,256]{1,0:T(8,128)(2,1)S(1)} %copy-done), kind=kOutput, calls=%fused_computation.65 | convolution fusion | flops 6710886400 | bytes 31457280 | tf_op jit(solution)/shard_map/dot_general | solution.py:35
  23.8 15.1 %fusion.25 = f32[5120,256]{1,0:T(8,128)} fusion(bf16[2560,5120]{1,0:T(8,128)(2,1)} %param.4, bf16[2560,256]{1,0:T(8,128)(2,1)S(1)} %copy-done.10), kind=kOutput, calls=%fused_computation.67 | convolution fusion | flops 6710886400 | bytes 32768000 | tf_op jit(solution)/shard_map/dot_general | solution.py:37
  38.8 90.6 %all-reduce.8.cloned.1.call-done = f32[2560,256]{1,0:T(8,128)} async-done(((f32[2560,256]{1,0:T(8,128)}), f32[2560,256]{1,0:T(8,128)}) %all-reduce.8.cloned.1.call-update) | async-done | bytes 2621456 | tf_op jit(solution)/shard_map/psum | solution.py:36
  129.4 7.5 %fusion.24 = f32[256,256]{0,1:T(8,128)} fusion(f32[2560,256]{1,0:T(8,128)} %all-reduce.8.cloned.1.call-done), kind=kOutput, calls=%fused_computation.66 | convolution fusion | flops 2013265920 | bytes 2883584 | tf_op jit(solution)/shard_map/dot_general | solution.py:10
  137.2 94.2 %all-reduce.16.cloned.1.call-done = (f32[5120,256]{1,0:T(8,128)}, f32[256,256]{0,1:T(8,128)}) async-done(((f32[5120,256]{1,0:T(8,128)}, f32[256,256]{0,1:T(8,128)}), (f32[5120,256]{1,0:T(8,128)}, f32[256,256]{0,1:T(8,128)})) %all-reduce.16.cloned.1.call-update) | async-done | bytes 5505040 | tf_op jit(solution)/shard_map/psum | solution.py:40
  231.4 13.1 %fusion.26 = f32[256,256]{0,1:T(8,128)} fusion(f32[5120,256]{1,0:T(8,128)} %get-tuple-element.35), kind=kOutput, calls=%fused_computation.68 | convolution fusion | flops 4026531840 | bytes 5505024 | tf_op jit(solution)/shard_map/dot_general | solution.py:10
  245.3 11.7 %cholesky.130 = f32[128,128]{1,0:T(8,128)S(1)} custom-call(f32[128,128]{1,0:T(8,128)S(1)} %cholesky.194), custom_call_target="Cholesky" | custom-call | tf_op jit(solution)/shard_map/jit(cholesky)/cholesky | solution.py:20
  257.0 10.4 %custom-call.19 = f32[1,128,128]{1,2,0:T(8,128)} custom-call(f32[1,128,128]{2,1,0:T(8,128)S(1)} %get-tuple-element.44), custom_call_target="InvertDiagBlocksLowerTriangular" | custom-call | tf_op jit(solution)/shard_map/jit(cholesky)/cholesky | solution.py:20
  267.5 12.9 %all-reduce.10.cloned.1.call-done = f32[256,256]{0,1:T(8,128)} async-done(((f32[256,256]{0,1:T(8,128)}), f32[256,256]{0,1:T(8,128)}) %all-reduce.10.cloned.1.call-update) | async-done | bytes 262160 | tf_op jit(solution)/shard_map/psum | solution.py:42
  282.5 11.7 %cholesky.164 = f32[128,128]{1,0:T(8,128)S(1)} custom-call(f32[128,128]{1,0:T(8,128)S(1)} %cholesky.197), custom_call_target="Cholesky" | custom-call | tf_op jit(solution)/shard_map/jit(cholesky)/cholesky | solution.py:20
  294.2 10.0 %custom-call.20 = f32[1,128,128]{1,2,0:T(8,128)S(1)} custom-call(f32[1,128,128]{2,1,0:T(8,128)S(1)} %get-tuple-element.48), custom_call_target="InvertDiagBlocksLowerTriangular" | custom-call | tf_op jit(solution)/shard_map/jit(cholesky)/cholesky | solution.py:20
  304.7 11.7 %cholesky.181 = f32[128,128]{1,0:T(8,128)S(1)} custom-call(f32[128,128]{1,0:T(8,128)S(1)} %convolution_subtract_fusion.2), custom_call_target="Cholesky" | custom-call | tf_op jit(solution)/shard_map/jit(cholesky)/cholesky | solution.py:20
  318.5 4.0 while.3
  319.1 1.4 bitcast_dynamic-update-slice_fusion.5
  321.1 1.4 bitcast_dynamic-update-slice_fusion.5
  322.5 19.7 %custom-call.17 = f32[2,128,128]{1,2,0:T(8,128)S(1)} custom-call(f32[2,128,128]{2,1,0:T(8,128)S(1)} %get-tuple-element.18), custom_call_target="InvertDiagBlocksLowerTriangular" | custom-call | tf_op jit(solution)/shard_map/jit(_solve_triangular)/triangular_solve | solution.py:21
  342.2 5.4 fusion.21
  347.6 4.4 convolution_subtract_fusion
  352.1 2.4 convolution_convert_fusion
  355.6 13.7 %convolution_bitcast_fusion = f32[2560,256]{0,1:T(8,128)} fusion(bf16[2560,5120]{1,0:T(8,128)(2,1)} %param.4, bf16[128,5120]{1,0:T(8,128)(2,1)S(1)} %convolution_convert_fusion, bf16[128,5120]{1,0:T(8,128)(2,1)S(1)} %copy-done.4), kind=kOutput, calls=%fused_computation.7 | convolution fusion | flops 6716129280 | bytes 31457280 | tf_op jit(solution)/shard_map/dot_general | solution.py:45
  369.8 11.7 %cholesky.147 = f32[128,128]{1,0:T(8,128)S(1)} custom-call(f32[128,128]{1,0:T(8,128)S(1)} %convolution_subtract_fusion.3), custom_call_target="Cholesky" | custom-call | tf_op jit(solution)/shard_map/jit(cholesky)/cholesky | solution.py:20
  383.5 4.1 while.2
  386.3 1.3 bitcast_dynamic-update-slice_fusion.4
  387.6 20.3 %custom-call.16 = f32[2,128,128]{1,2,0:T(8,128)} custom-call(f32[2,128,128]{2,1,0:T(8,128)S(1)} %get-tuple-element.10), custom_call_target="InvertDiagBlocksLowerTriangular" | custom-call | tf_op jit(solution)/shard_map/jit(_solve_triangular)/triangular_solve | solution.py:21
  407.9 2.1 fusion.22
  410.1 2.2 convolution_subtract_fusion.1
  413.6 59.9 %all-reduce.12.cloned.1.call-done = f32[2560,256]{0,1:T(8,128)} async-done(((f32[2560,256]{0,1:T(8,128)}), f32[2560,256]{0,1:T(8,128)}) %all-reduce.12.cloned.1.call-update) | async-done | bytes 2621456 | tf_op jit(solution)/shard_map/psum | solution.py:46
  473.5 3.9 fusion.4
  477.3 53.1 %all-reduce.14.cloned.1.call-done = f32[256,256]{1,0:T(8,128)} async-done(((f32[256,256]{1,0:T(8,128)}), f32[256,256]{1,0:T(8,128)}) %all-reduce.14.cloned.1.call-update) | async-done | bytes 262160 | tf_op jit(solution)/shard_map/psum | solution.py:47
  530.4 3.5 convolution_convert_fusion.1
  533.9 22.9 %subtract_convert_fusion = bf16[2560,5120]{1,0:T(8,128)(2,1)} fusion(bf16[2560,5120]{1,0:T(8,128)(2,1)} %param.4, bf16[2560,256]{1,0:T(8,128)(2,1)} %convolution_convert_fusion.1, bf16[128,5120]{1,0:T(8,128)(2,1)} %copy-done.5, bf16[128,5120]{1,0:T(8,128)(2,1)} %get-tuple-element.51), kind=kOutput, calls=%fused_computation.4 | convolution fusion | flops 6755450880 | bytes 56360960 | tf_op jit(solution)/shard_map/dot_general | solution.py:55
  (66 shorter events, 13.8 us)
Async XLA Ops:
  7.2 1.7 copy-start
  7.2 122.2 %all-reduce.8.cloned.1.call-start = ((), (), s32[]{:S(2)}) async-start(), calls=%async_computation | async-start | bytes 5242880 | tf_op jit(solution)/shard_map/psum | solution.py:36
  22.4 1.3 copy-start.10
  22.5 208.9 %all-reduce.16.cloned.1.call-start = ((), (), s32[]{:S(2)}) async-start(), calls=%async_computation.4 | async-start | bytes 11010048 | tf_op jit(solution)/shard_map/psum | solution.py:40
  136.9 143.4 %all-reduce.10.cloned.1.call-start = ((), (), s32[]{:S(2)}) async-start(), calls=%async_computation.1 | async-start | bytes 524288 | tf_op jit(solution)/shard_map/psum | solution.py:42
  231.4 13.7 %copy-start.6 = (f32[256,256]{0,1:T(8,128)S(1)}, f32[256,256]{0,1:T(8,128)}, u32[]{:S(2)}) copy-start(f32[256,256]{0,1:T(8,128)} %get-tuple-element.36) | copy-start | bytes 786436
  244.6 228.9 %all-reduce.12.cloned.1.call-start = ((), (), s32[]{:S(2)}) async-start(), calls=%async_computation.2 | async-start | bytes 5242880 | tf_op jit(solution)/shard_map/psum | solution.py:46
  342.2 5.4 copy-start.2
  352.1 3.5 copy-start.4
  354.5 1.1 copy-start.5
  355.6 13.8 %copy-start.9 = (f32[1,128,128]{1,2,0:T(8,128)S(1)}, f32[1,128,128]{1,2,0:T(8,128)}, u32[]{:S(2)}) copy-start(f32[1,128,128]{1,2,0:T(8,128)} %custom-call.19) | copy-start | bytes 196612
  369.3 38.6 %copy-start.3 = (f32[2560,256]{1,0:T(8,128)S(1)}, f32[2560,256]{1,0:T(8,128)}, u32[]{:S(2)}) copy-start(f32[2560,256]{1,0:T(8,128)} %all-reduce.8.cloned.1.call-done) | copy-start | bytes 7864324
  369.3 161.1 %all-reduce.14.cloned.1.call-start = ((), (), s32[]{:S(2)}) async-start(), calls=%async_computation.3 | async-start | bytes 524288 | tf_op jit(solution)/shard_map/psum | solution.py:47
  410.0 2.2 copy-start.8
  533.9 22.9 %copy-start.7 = (f32[256,256]{1,0:T(8,128)S(1)}, f32[256,256]{1,0:T(8,128)}, u32[]{:S(2)}) copy-start(f32[256,256]{1,0:T(8,128)} %all-reduce.14.cloned.1.call-done) | copy-start | bytes 786436
  533.9 23.6 %copy-start.1 = (bf16[5120,256]{1,0:T(8,128)(2,1)S(1)}, bf16[5120,256]{1,0:T(8,128)(2,1)}, u32[]{:S(2)}) copy-start(bf16[5120,256]{1,0:T(8,128)(2,1)} %param.5) | copy-start | bytes 7864324
Sparse Core Ops, SparseCore 0:
  22.6 106.7 all-reduce.7
  137.1 94.2 all-reduce.15
  244.7 35.6 all-reduce.9
  369.4 103.9 all-reduce.11
  477.5 52.9 all-reduce.13
where the time goes:
time: 573 us; the launch traced here: 565 us
  waiting for transfers between devices  311 us (54%)
  matrix products  112 us (20%)
  other arithmetic  110 us (19%)
  between operations  17 us (3%)
  local copies, waits for them, and re-layouts  13.1 us (2%)
    psum x1, waiting for transfers between devices, body(): sketch_cols = lax.psum(sketch_cols, 'row')  94.2 us
    psum x1, waiting for transfers between devices, body(): sketch_rows = lax.psum(sketch_rows, 'col')  90.6 us
    another operation x12, other arithmetic, orthonormal(): lower_factor = jnp.linalg.cholesky(gram_total)  68.7 us
    psum x1, waiting for transfers between devices, body(): applied = lax.psum(applied, 'col')  59.9 us
    psum x1, waiting for transfers between devices, body(): core_matrix = lax.psum(core_part(basis_rows, applied), 'row')  53.1 us
    another operation x5, other arithmetic, orthonormal(): jax.scipy.linalg.solve_triangular(lower_factor, sketch.T, lower=True)  40 us
    dot_general x1, matrix products, body(): lax.dot_general(projected, basis_cols, (((1,), (1,)), ((), ())), preferre...  22.9 us
    dot_general x2, matrix products, gram_matrix(): lax.dot_general(sketch, sketch, (((0,), (0,)), ((), ())), precision=lax.P...  20.6 us
  transfers between devices with their start and end apart: 5, of which 5 were waited for; matrix products, arithmetic and copies ran while one was open for 14% of the time, Pallas kernels for 0%

commit v1 on v0

--- a/solution.py
+++ b/solution.py
@@ -4,6 +4,17 @@
 from jax.sharding import PartitionSpec as P
 
 ORDER = 20480
+
+
+def wrap_the_domain(my_tile, device_axis):
+    n_slots = jax.lax.axis_size(device_axis)
+    z = lambda back: [(dev, dev ^ back) for dev in range(n_slots)]
+    tmp = my_tile
+    for p in range(n_slots.bit_length() - 1):
+        r2 = z(1 << p)
+        v_now = jax.lax.ppermute(tmp, device_axis, r2)
+        tmp = tmp + v_now
+    return tmp
 
 
 def gram_matrix(sketch):
@@ -33,7 +44,7 @@
 
 def body(front_matrix, right_samples, left_samples):
     sketch_rows = jnp.dot(front_matrix, right_samples, preferred_element_type=jnp.float32)
-    sketch_rows = lax.psum(sketch_rows, "col")
+    sketch_rows = wrap_the_domain(sketch_rows, "col")
     sketch_cols = lax.dot_general(
         front_matrix, left_samples, (((0,), (0,)), ((), ())), preferred_element_type=jnp.float32
     )

time: 573 us -> 642 us (1.12)
  waiting for transfers between devices: 311 us -> 372 us
    ppermute x0 -> x2, waiting for transfers between devices: none -> 155 us  [wrap_the_domain(): v_now = jax.lax.ppermute(tmp, device_axis, r2)]
    psum x1 -> x0, waiting for transfers between devices: 90.6 us -> none  [body(): sketch_rows = lax.psum(sketch_rows, 'col')]
  transfers between devices with their start and end apart: 5 -> 6, of which waited for: 5 -> 6; matrix products, arithmetic and copies ran while one was open for 14% -> 13% of each run, Pallas kernels for 0% -> 0%
where the time goes in v1:
time: 642 us; the launch traced here: 633 us
  waiting for transfers between devices  372 us (58%)
  other arithmetic  114 us (18%)
  matrix products  109 us (17%)
  between operations  17.1 us (3%)
  local copies, waits for them, and re-layouts  13.5 us (2%)
  starting transfers between devices  6.78 us (1%)
    ppermute x2, waiting for transfers between devices, wrap_the_domain(): v_now = jax.lax.ppermute(tmp, device_axis, r2)  155 us
    psum x1, waiting for transfers between devices, body(): sketch_cols = lax.psum(sketch_cols, 'row')  92.6 us
    another operation x12, other arithmetic, orthonormal(): lower_factor = jnp.linalg.cholesky(gram_total)  68.8 us
    psum x1, waiting for transfers between devices, body(): applied = lax.psum(applied, 'col')  58.7 us
    psum x1, waiting for transfers between devices, body(): core_matrix = lax.psum(core_part(basis_rows, applied), 'row')  53.1 us
    another operation x5, other arithmetic, orthonormal(): jax.scipy.linalg.solve_triangular(lower_factor, sketch.T, lower=True)  40 us
    dot_general x1, matrix products, body(): lax.dot_general(projected, basis_cols, (((1,), (1,)), ((), ())), preferre...  22.9 us
    another operation x6, matrix products, orthonormal(): jax.scipy.linalg.solve_triangular(lower_factor, sketch.T, lower=True)  18.8 us
  transfers between devices with their start and end apart: 6, of which 6 were waited for; matrix products, arithmetic and copies ran while one was open for 13% of the time, Pallas kernels for 0%

profile of v1, /device:TPU:0, one launch (start us, length us, event | category | flops | bytes accessed | tf_op | source)
XLA Modules:
  0.0 633.3 jit_solution(5908044176676782673)
XLA Ops:
  8.9 12.3 %fusion.26 = f32[2560,256]{1,0:T(8,128)S(1)} fusion(bf16[2560,5120]{1,0:T(8,128)(2,1)} %param.4, bf16[5120,256]{1,0:T(8,128)(2,1)S(1)} %copy-done), kind=kOutput, calls=%fused_computation.69 | convolution fusion | flops 6710886400 | bytes 31457280 | tf_op jit(solution)/shard_map/dot_general | solution.py:46
  21.2 3.1 collective-permute-start
  24.3 56.9 %collective-permute-done = f32[2560,256]{1,0:T(8,128)S(1)} collective-permute-done((f32[2560,256]{1,0:T(8,128)S(1)}, f32[2560,256]{1,0:T(8,128)S(1)}, u32[]{:S(2)}, u32[]{:S(2)}) %collective-permute-start) | collective-permute-done | bytes 2621472 | tf_op jit(solution)/shard_map/ppermute | solution.py:15
  81.5 2.8 collective-permute-start.1
  84.3 14.7 %fusion.27 = f32[5120,256]{1,0:T(8,128)} fusion(bf16[2560,5120]{1,0:T(8,128)(2,1)} %param.4, bf16[2560,256]{1,0:T(8,128)(2,1)S(1)} %copy-done.12), kind=kOutput, calls=%fused_computation.70 | convolution fusion | flops 6710886400 | bytes 32768000 | tf_op jit(solution)/shard_map/dot_general | solution.py:48
  99.0 97.7 %collective-permute-done.1 = f32[2560,256]{1,0:T(8,128)S(1)} collective-permute-done((f32[2560,256]{1,0:T(8,128)S(1)}, f32[2560,256]{1,0:T(8,128)S(1)}, u32[]{:S(2)}, u32[]{:S(2)}) %collective-permute-start.1) | collective-permute-done | bytes 2621472 | tf_op jit(solution)/shard_map/ppermute | solution.py:15
  198.2 5.2 fusion.4
  203.7 3.6 add_bitcast_fusion
  207.3 92.6 %all-reduce.13.cloned.1.call-done = (f32[5120,256]{1,0:T(8,128)}, f32[256,256]{0,1:T(8,128)}) async-done(((f32[5120,256]{1,0:T(8,128)}, f32[256,256]{0,1:T(8,128)}), (f32[5120,256]{1,0:T(8,128)}, f32[256,256]{0,1:T(8,128)})) %all-reduce.13.cloned.1.call-update) | async-done | bytes 5505040 | tf_op jit(solution)/shard_map/psum | solution.py:51
  299.9 13.1 %fusion.28 = f32[256,256]{0,1:T(8,128)} fusion(f32[5120,256]{1,0:T(8,128)} %get-tuple-element.35), kind=kOutput, calls=%fused_computation.71 | convolution fusion | flops 4026531840 | bytes 5505024 | tf_op jit(solution)/shard_map/dot_general | solution.py:21
  313.8 11.7 %cholesky.130 = f32[128,128]{1,0:T(8,128)S(1)} custom-call(f32[128,128]{1,0:T(8,128)S(1)} %cholesky.194), custom_call_target="Cholesky" | custom-call | tf_op jit(solution)/shard_map/jit(cholesky)/cholesky | solution.py:31
  325.5 10.4 %custom-call.19 = f32[1,128,128]{1,2,0:T(8,128)} custom-call(f32[1,128,128]{2,1,0:T(8,128)S(1)} %get-tuple-element.44), custom_call_target="InvertDiagBlocksLowerTriangular" | custom-call | tf_op jit(solution)/shard_map/jit(cholesky)/cholesky | solution.py:31
  336.0 12.9 %all-reduce.7.cloned.1.call-done = f32[256,256]{0,1:T(8,128)} async-done(((f32[256,256]{0,1:T(8,128)}), f32[256,256]{0,1:T(8,128)}) %all-reduce.7.cloned.1.call-update) | async-done | bytes 262160 | tf_op jit(solution)/shard_map/psum | solution.py:53
  351.0 11.7 %cholesky.164 = f32[128,128]{1,0:T(8,128)S(1)} custom-call(f32[128,128]{1,0:T(8,128)S(1)} %cholesky.197), custom_call_target="Cholesky" | custom-call | tf_op jit(solution)/shard_map/jit(cholesky)/cholesky | solution.py:31
  362.8 10.0 %custom-call.20 = f32[1,128,128]{1,2,0:T(8,128)S(1)} custom-call(f32[1,128,128]{2,1,0:T(8,128)S(1)} %get-tuple-element.48), custom_call_target="InvertDiagBlocksLowerTriangular" | custom-call | tf_op jit(solution)/shard_map/jit(cholesky)/cholesky | solution.py:31
  373.2 11.7 %cholesky.181 = f32[128,128]{1,0:T(8,128)S(1)} custom-call(f32[128,128]{1,0:T(8,128)S(1)} %convolution_subtract_fusion.1), custom_call_target="Cholesky" | custom-call | tf_op jit(solution)/shard_map/jit(cholesky)/cholesky | solution.py:31
  387.1 4.0 while.3
  391.1 19.7 %custom-call.17 = f32[2,128,128]{1,2,0:T(8,128)S(1)} custom-call(f32[2,128,128]{2,1,0:T(8,128)S(1)} %get-tuple-element.18), custom_call_target="InvertDiagBlocksLowerTriangular" | custom-call | tf_op jit(solution)/shard_map/jit(_solve_triangular)/triangular_solve | solution.py:32
  410.8 5.4 fusion.24
  416.2 4.4 convolution_subtract_fusion
  420.6 2.4 convolution_convert_fusion
  424.1 13.7 %convolution_bitcast_fusion = f32[2560,256]{0,1:T(8,128)} fusion(bf16[2560,5120]{1,0:T(8,128)(2,1)} %param.4, bf16[128,5120]{1,0:T(8,128)(2,1)S(1)} %convolution_convert_fusion, bf16[128,5120]{1,0:T(8,128)(2,1)S(1)} %copy-done.6), kind=kOutput, calls=%fused_computation.7 | convolution fusion | flops 6716129280 | bytes 31457280 | tf_op jit(solution)/shard_map/dot_general | solution.py:56
  438.3 11.7 %cholesky.147 = f32[128,128]{1,0:T(8,128)S(1)} custom-call(f32[128,128]{1,0:T(8,128)S(1)} %convolution_subtract_fusion.2), custom_call_target="Cholesky" | custom-call | tf_op jit(solution)/shard_map/jit(cholesky)/cholesky | solution.py:31
  452.1 4.2 while.2
  456.4 20.3 %custom-call.16 = f32[2,128,128]{1,2,0:T(8,128)} custom-call(f32[2,128,128]{2,1,0:T(8,128)S(1)} %get-tuple-element.10), custom_call_target="InvertDiagBlocksLowerTriangular" | custom-call | tf_op jit(solution)/shard_map/jit(_solve_triangular)/triangular_solve | solution.py:32
  476.7 2.2 fusion.25
  478.9 2.2 fusion.12
  483.3 58.7 %all-reduce.9.cloned.1.call-done = f32[2560,256]{0,1:T(8,128)} async-done(((f32[2560,256]{0,1:T(8,128)}), f32[2560,256]{0,1:T(8,128)}) %all-reduce.9.cloned.1.call-update) | async-done | bytes 2621456 | tf_op jit(solution)/shard_map/psum | solution.py:57
  541.9 4.1 fusion.6
  546.1 53.1 %all-reduce.11.cloned.1.call-done = f32[256,256]{1,0:T(8,128)} async-done(((f32[256,256]{1,0:T(8,128)}), f32[256,256]{1,0:T(8,128)}) %all-reduce.11.cloned.1.call-update) | async-done | bytes 262160 | tf_op jit(solution)/shard_map/psum | solution.py:58
  599.1 3.5 convolution_convert_fusion.1
  602.6 22.9 %subtract_convert_fusion = bf16[2560,5120]{1,0:T(8,128)(2,1)} fusion(bf16[2560,5120]{1,0:T(8,128)(2,1)} %param.4, bf16[2560,256]{1,0:T(8,128)(2,1)} %convolution_convert_fusion.1, bf16[128,5120]{1,0:T(8,128)(2,1)} %copy-done.7, bf16[128,5120]{1,0:T(8,128)(2,1)} %get-tuple-element.51), kind=kOutput, calls=%fused_computation.4 | convolution fusion | flops 6755450880 | bytes 56360960 | tf_op jit(solution)/shard_map/dot_general | solution.py:66
  (73 shorter events, 21.2 us)
Async XLA Ops:
  7.2 1.7 copy-start
  7.2 292.7 %all-reduce.13.cloned.1.call-start = ((), (), s32[]{:S(2)}) async-start(), calls=%async_computation.3 | async-start | bytes 11010048 | tf_op jit(solution)/shard_map/psum | solution.py:51
  21.2 63.2 %copy-start.12 = (bf16[2560,256]{1,0:T(8,128)(2,1)S(1)}, bf16[2560,256]{1,0:T(8,128)(2,1)}, u32[]{:S(2)}) copy-start(bf16[2560,256]{1,0:T(8,128)(2,1)} %param.6) | copy-start | bytes 3932164
  21.2 60.0 %collective-permute-start = (f32[2560,256]{1,0:T(8,128)S(1)}, f32[2560,256]{1,0:T(8,128)S(1)}, u32[]{:S(2)}, u32[]{:S(2)}) collective-permute-start(f32[2560,256]{1,0:T(8,128)S(1)} %fusion.26), channel_id=1, source_target_pairs={{0,1},{1,0},{2,3},{3,2},{4,5},{5,4},{6,7},{7,6},{8,9},{9,8},{10,11... | collective-permute-start | bytes 7864328 | tf_op jit(solution)/shard_map/ppermute | solution.py:15
  81.5 115.2 %collective-permute-start.1 = (f32[2560,256]{1,0:T(8,128)S(1)}, f32[2560,256]{1,0:T(8,128)S(1)}, u32[]{:S(2)}, u32[]{:S(2)}) collective-permute-start(f32[2560,256]{1,0:T(8,128)S(1)} %add.38), channel_id=1, source_target_pairs={{0,2},{1,3},{2,0},{3,1},{4,6},{5,7},{6,4},{7,5},{8,10},{9,11},{10,... | collective-permute-start | bytes 7864328 | tf_op jit(solution)/shard_map/ppermute | solution.py:15
  196.7 1.5 copy-start.4
  203.4 145.5 %all-reduce.7.cloned.1.call-start = ((), (), s32[]{:S(2)}) async-start(), calls=%async_computation | async-start | bytes 524288 | tf_op jit(solution)/shard_map/psum | solution.py:53
  299.9 13.7 %copy-start.8 = (f32[256,256]{0,1:T(8,128)S(1)}, f32[256,256]{0,1:T(8,128)}, u32[]{:S(2)}) copy-start(f32[256,256]{0,1:T(8,128)} %get-tuple-element.36) | copy-start | bytes 786436
  313.1 228.9 %all-reduce.9.cloned.1.call-start = ((), (), s32[]{:S(2)}) async-start(), calls=%async_computation.1 | async-start | bytes 5242880 | tf_op jit(solution)/shard_map/psum | solution.py:57
  410.8 5.4 copy-start.2
  420.6 3.5 copy-start.6
  423.0 1.1 copy-start.7
  424.1 13.8 %copy-start.11 = (f32[1,128,128]{1,2,0:T(8,128)S(1)}, f32[1,128,128]{1,2,0:T(8,128)}, u32[]{:S(2)}) copy-start(f32[1,128,128]{1,2,0:T(8,128)} %custom-call.19) | copy-start | bytes 196612
  437.8 38.9 %copy-start.3 = (f32[256,2560]{0,1:T(8,128)S(1)}, f32[256,2560]{0,1:T(8,128)}, u32[]{:S(2)}) copy-start(f32[256,2560]{0,1:T(8,128)} %add_bitcast_fusion) | copy-start | bytes 7864324
  437.8 161.3 %all-reduce.11.cloned.1.call-start = ((), (), s32[]{:S(2)}) async-start(), calls=%async_computation.2 | async-start | bytes 524288 | tf_op jit(solution)/shard_map/psum | solution.py:58
  476.7 4.4 copy-start.10
  483.3 115.8 %copy-start.5 = (bf16[128,2560]{1,0:T(8,128)(2,1)S(1)}, bf16[128,2560]{1,0:T(8,128)(2,1)}, u32[]{:S(2)}) copy-start(bf16[128,2560]{1,0:T(8,128)(2,1)} %convolution_convert_fusion.2) | copy-start | bytes 1966084
  602.6 22.9 %copy-start.9 = (f32[256,256]{1,0:T(8,128)S(1)}, f32[256,256]{1,0:T(8,128)}, u32[]{:S(2)}) copy-start(f32[256,256]{1,0:T(8,128)} %all-reduce.11.cloned.1.call-done) | copy-start | bytes 786436
  602.6 23.6 %copy-start.1 = (bf16[5120,256]{1,0:T(8,128)(2,1)S(1)}, bf16[5120,256]{1,0:T(8,128)(2,1)}, u32[]{:S(2)}) copy-start(bf16[5120,256]{1,0:T(8,128)(2,1)} %param.5) | copy-start | bytes 7864324
Sparse Core Ops, SparseCore 0:
  203.6 96.2 all-reduce.12
  313.2 35.6 all-reduce.6
  437.9 103.9 all-reduce.8
  546.2 52.8 all-reduce.10
